TPU v7x, 256 devices: a whole 4x4x8 slice. The times are simulated.
256 devices in a mesh: layer: 4 (over y), row: 8 (over x, core), col: 8 (over z).
Axes of the slice: x: 4, y: 4, z: 8, core: 2. Of those that a mesh axis runs over, the one named last changes fastest.
Arguments:
- l_blocks: bfloat16 [4, 64, 256, 256], P('layer', ('row', 'col')), may hold values from -3 to 3
- l_ids: int32 [4, 64], P('layer'), may hold values from 0 to 127, as said below
- u_blocks: bfloat16 [4, 64, 256, 256], P('layer', ('row', 'col')), may hold values from -3 to 3
- u_ids: int32 [4, 64], P('layer'), may hold values from 0 to 127, as said below
- inv_upper: bfloat16 [8, 256, 256], replicated, as said below
- inv_lower: bfloat16 [8, 256, 256], replicated, as said below
- row_order: int32 [16], replicated, may hold values from 0 to 15, as said below
- col_order: int32 [16], replicated, may hold values from 0 to 15, as said below
- front_in: float32 [16, 16, 256, 256], P('row', 'col', 'layer'), may hold values from -6 to 6
- leaf_lower: bfloat16 [256, 1024, 1024], P(('layer', 'row', 'col')), may hold values from -6 to 6
- leaf_upper: bfloat16 [256, 1024, 1024], P(('layer', 'row', 'col')), may hold values from -0.1875 to 0.1875
- leaf_front: bfloat16 [256, 1024, 1024], P(('layer', 'row', 'col')), may hold values from -6 to 6
Outputs:
- front_out: float32 [16, 16, 256, 256], P('row', 'col', 'layer')
- leaf_out: bfloat16 [256, 1024, 1024], P(('layer', 'row', 'col'))
Inputs may be any that keep to these rules, and one draw needn't show every extreme that they name: `l_ids`: within a layer the ids are distinct; the entry at index r * 8 + c has i = row_order[r * 2 + p] for some p < 2. `u_ids`: within a layer the ids are distinct; the entry at index r * 8 + c has j = col_order[c * 2 + q] for some q < 2. `row_order`: A permutation of the tile rows. `col_order`: A permutation of the tile columns. `inv_upper`: each block is upper triangular with a positive diagonal. `inv_lower`: each block is lower triangular with a positive diagonal.
All inputs are finite; a program needn't handle non-finite values.
Results may differ from a plain program's by a relative error of at most 0.0095.
Values may be sent and summed in bfloat16 or wider, within the bound.
No kernel may reach another device: no remote copies, remote signals or barrier semaphores. Data moves between devices by JAX's collectives and lax.ppermute only.
A program may use at most 128 MiB of HBM per device.

v0:
```python
import jax
import jax.numpy as jnp
from jax import lax
from jax.sharding import PartitionSpec as P


def place_all(carry, blocks, ids, wanted):
    matches = wanted[:, :, None] == ids[None, None, :]
    present = jnp.any(matches, axis=2)
    position = jnp.argmax(matches.astype(jnp.int32), axis=2)
    picked = blocks[position]
    return jnp.where(present[:, :, None, None], picked, carry)


def shards(
    l_blocks,
    l_ids,
    u_blocks,
    u_ids,
    inv_upper,
    inv_lower,
    row_order,
    col_order,
    front_in,
    leaf_lower,
    leaf_upper,
    leaf_front,
):
    tile = l_blocks.shape[-1]
    panel_count = inv_upper.shape[0]
    tiles_side = row_order.shape[0]
    rows_owned = front_in.shape[0]
    cols_owned = front_in.shape[1]
    grid_row = lax.axis_index("row")
    grid_col = lax.axis_index("col")
    col_count = lax.axis_size("col")
    lower_ids = l_ids[0]
    upper_ids = u_ids[0]
    place = grid_row * col_count + grid_col
    my_lower = lower_ids[place]
    my_upper = upper_ids[place]
    inv_u = lax.dynamic_index_in_dim(inv_upper, my_lower % panel_count, 0, keepdims=False)
    inv_l = lax.dynamic_index_in_dim(inv_lower, my_upper // tiles_side, 0, keepdims=False)
    lower = jnp.dot(l_blocks[0, 0], inv_u, preferred_element_type=jnp.float32).astype(jnp.bfloat16)
    upper = jnp.dot(inv_l, u_blocks[0, 0], preferred_element_type=jnp.float32).astype(jnp.bfloat16)
    owned_rows = lax.dynamic_slice_in_dim(row_order, grid_row * rows_owned, rows_owned)
    owned_cols = lax.dynamic_slice_in_dim(col_order, grid_col * cols_owned, cols_owned)
    panel = jnp.arange(panel_count, dtype=jnp.int32)
    want_lower = owned_rows[:, None] * panel_count + panel[None, :]
    want_upper = panel[:, None] * tiles_side + owned_cols[None, :]
    empty_lower = jnp.zeros((rows_owned, panel_count, tile, tile), jnp.bfloat16)
    empty_upper = jnp.zeros((panel_count, cols_owned, tile, tile), jnp.bfloat16)
    low_sel = place_all(
        empty_lower,
        lax.all_gather(lower[None], ("row", "col"), axis=0, tiled=True),
        lower_ids,
        want_lower,
    )
    up_sel = place_all(
        empty_upper,
        lax.all_gather(upper[None], ("row", "col"), axis=0, tiled=True),
        upper_ids,
        want_upper,
    )
    schur = jnp.einsum("pkab,kqbc->pqac", low_sel, up_sel, preferred_element_type=jnp.float32)
    summed = lax.psum_scatter(
        schur.astype(jnp.bfloat16), "layer", scatter_dimension=2, tiled=True
    ).astype(jnp.float32)
    front_out = front_in - summed
    update = jnp.dot(leaf_lower[0], leaf_upper[0], preferred_element_type=jnp.float32)
    leaf_out = (leaf_front[0].astype(jnp.float32) - update).astype(jnp.bfloat16)[None]
    return (front_out, leaf_out)


def solution(mesh):
    return jax.shard_map(
        shards,
        mesh=mesh,
        in_specs=(
            P("layer", ("row", "col"), None, None),
            P("layer", None),
            P("layer", ("row", "col"), None, None),
            P("layer", None),
            P(),
            P(),
            P(),
            P(),
            P("row", "col", "layer", None),
            P(("layer", "row", "col"), None, None),
            P(("layer", "row", "col"), None, None),
            P(("layer", "row", "col"), None, None),
        ),
        out_specs=(P("row", "col", "layer", None), P(("layer", "row", "col"), None, None)),
        check_vma=False,
    )
```

profile of v0, /device:TPU:2, one launch (start us, length us, event | category | flops | bytes accessed | tf_op | source)
XLA Modules:
  0.0 250.7 jit_solution(5410724124969795494)
XLA Ops:
  7.2 0.0 copy-start
  7.2 0.0 all-gather.7.cloned.1.call-start
  7.2 1.4 constant_dynamic-slice_fusion
  10.6 1.9 fusion.29
  12.4 0.0 all-gather.7.cloned.1.call-update
  12.5 0.0 all-gather.5.cloned.1.call-start
  15.1 1.8 convolution_convert_fusion.1
  16.9 0.0 all-gather.5.cloned.1.call-update
  17.0 0.0 all-reduce.3.cloned.1.call-start
  17.0 0.7 dynamic-slice_multiply_fusion
  17.8 0.1 iota_add_fusion
  17.8 1.4 fusion.38
  19.2 0.1 reshape.78
  19.3 0.7 dynamic_slice.19
  20.1 0.1 broadcast_add_fusion
  20.1 1.4 fusion.37
  21.5 0.1 copy.27
  21.6 0.1 reshape.70
  21.7 0.9 compare_reduce_fusion.1
  22.6 0.1 copy.26
  22.7 1.3 dynamic-slice.2
  24.6 0.9 compare_reduce_fusion
  25.5 75.3 %all-gather.7.cloned.1.call-done = bf16[16384,256]{0,1:T(8,128)(2,1)} async-done(((bf16[256,256]{0,1:T(8,128)(2,1)}), bf16[16384,256]{0,1:T(8,128)(2,1)}) %all-gather.7.cloned.1.call-update) | async-done | bytes 8388624 | tf_op jit(solution)/shard_map/all_gather | solution.py:55
  100.8 11.9 %copy.37 = bf16[16384,256]{1,0:T(8,128)(2,1)} copy(bf16[16384,256]{0,1:T(8,128)(2,1)} %all-gather.7.cloned.1.call-done) | data formatting | bytes 16777216 | tf_op jit(solution)/shard_map/all_gather | solution.py:55
  112.7 5.4 %gather_fusion.1 = bf16[16,256,256]{2,1,0:T(8,128)(2,1)} fusion(bf16[64,256,256]{2,1,0:T(8,128)(2,1)} %bitcast.60, s32[1024]{0:T(1024)S(1)} %pad_clamp_fusion), kind=kCustom, calls=%fused_computation.1 | custom fusion | bytes 4194368 | tf_op jit(solution)/shard_map/gather | solution.py:11
  118.1 67.2 %all-gather.5.cloned.1.call-done = bf16[16384,256]{1,0:T(8,128)(2,1)} async-done(((bf16[256,256]{1,0:T(8,128)(2,1)}), bf16[16384,256]{1,0:T(8,128)(2,1)}) %all-gather.5.cloned.1.call-update) | async-done | bytes 8388624 | tf_op jit(solution)/shard_map/all_gather | solution.py:61
  185.4 5.5 %gather_fusion = bf16[16,256,256]{2,1,0:T(8,128)(2,1)} fusion(bf16[64,256,256]{2,1,0:T(8,128)(2,1)} %bitcast.63, s32[1024]{0:T(1024)S(1)} %pad_clamp_fusion.1), kind=kCustom, calls=%fused_computation | custom fusion | bytes 4194368 | tf_op jit(solution)/shard_map/gather | solution.py:11
  190.8 3.7 %fusion.24 = bf16[2,2,256,256]{2,3,0,1:T(8,128)(2,1)S(1)} fusion(bf16[2,8,256,256]{3,2,1,0:T(8,128)(2,1)} %bitcast.61, pred[2,8]{1,0:T(4,128)(4,1)S(1)} %compare_reduce_fusion, bf16[8,2,256,256]{3,2,1,0:T(8,128)(2,1)} %bitcast.62, pred[8,2]{1,0:T(8,128)(4,1)S(1)} %copy.26), kind=kOutput, calls=%fused_computation.16 | convolution fusion | flops 1076101120 | bytes 4718624 | tf_op jit(solution)/shard_map/pkab,kqbc->pqac/dot_general | solution.py:65
  194.5 1.2 copy.30
  195.7 0.0 all-reduce.3.cloned.1.call-update
  195.7 0.0 copy-done
  195.7 0.0 copy-start.1
  195.8 5.9 %fusion.1 = bf16[1,1024,1024]{2,1,0:T(8,128)(2,1)} fusion(bf16[1,1024,1024]{2,1,0:T(8,128)(2,1)} %param.23, bf16[1,1024,1024]{2,1,0:T(8,128)(2,1)S(1)} %copy-done, bf16[1,1024,1024]{2,1,0:T(8,128)(2,1)} %param.21), kind=kOutput, calls=%fused_computation.4 | convolution fusion | flops 2150629376 | bytes 8388608 | tf_op jit(solution)/shard_map/dot_general | solution.py:70
  201.7 40.5 %all-reduce.3.cloned.1.call-done = bf16[2,2,256,256]{3,1,0,2:T(2,128)(2,1)} async-done(((bf16[2,2,256,256]{3,1,0,2:T(2,128)(2,1)}), bf16[2,2,256,256]{3,1,0,2:T(2,128)(2,1)}) %all-reduce.3.cloned.1.call-update) | async-done | bytes 524304
  242.2 0.0 copy-done.1
  242.2 1.2 copy_subtract_fusion
  243.4 0.8 copy.32
  (5 shorter events, 0.0 us)
Async XLA Ops:
  7.2 188.6 %copy-start = (bf16[1,1024,1024]{2,1,0:T(8,128)(2,1)S(1)}, bf16[1,1024,1024]{2,1,0:T(8,128)(2,1)}, u32[]{:S(2)}) copy-start(bf16[1,1024,1024]{2,1,0:T(8,128)(2,1)} %param.22) | copy-start | bytes 6291460
  7.2 93.6 %all-gather.7.cloned.1.call-start = ((), (), s32[]{:S(2)}) async-start(), calls=%async_computation.1 | async-start | bytes 8519680 | tf_op jit(solution)/shard_map/all_gather | solution.py:55
  12.5 172.9 %all-gather.5.cloned.1.call-start = ((), (), s32[]{:S(2)}) async-start(), calls=%async_computation | async-start | bytes 8519680 | tf_op jit(solution)/shard_map/all_gather | solution.py:61
  17.0 225.2 %all-reduce.3.cloned.1.call-start = ((), (), s32[]{:S(2)}) async-start(), calls=%async_computation.2 | async-start | bytes 1048576
  195.7 46.5 %copy-start.1 = (f32[2,2,64,256]{3,2,1,0:T(8,128)S(1)}, f32[2,2,64,256]{3,2,1,0:T(8,128)}, u32[]{:S(2)}) copy-start(f32[2,2,64,256]{3,2,1,0:T(8,128)} %param.20) | copy-start | bytes 786436
Sparse Core Ops, SparseCore 0:
  12.6 88.1 all-gather.6
  103.5 81.7 all-gather.4
  195.8 46.3 all-reduce.2
where the time goes:
time: 251 us
  waiting for transfers between devices  183 us (73%)
  local copies, waits for them, and re-layouts  28.5 us (11%)
  between operations  19 us (8%)
  matrix products  13.3 us (5%)
  other arithmetic  6.61 us (3%)
    all_gather x1, waiting for transfers between devices, shards(): lax.all_gather(lower[None], ('row', 'col'), axis=0, tiled=True)  75.3 us
    all_gather x1, waiting for transfers between devices, shards(): lax.all_gather(upper[None], ('row', 'col'), axis=0, tiled=True)  67.2 us
    unnamed x4, waiting for transfers between devices  40.6 us
    all_gather x1, local copies, waits for them, and re-layouts, shards(): lax.all_gather(lower[None], ('row', 'col'), axis=0, tiled=True)  11.9 us
    gather x2, local copies, waits for them, and re-layouts, place_all(): picked = blocks[position]  10.9 us
    dot_general x1, matrix products, shards(): jnp.dot(leaf_lower[0], leaf_upper[0], preferred_element_type=jnp.float32)  5.92 us
  transfers between devices with their start and end apart: 3, of which 3 were waited for; matrix products, arithmetic and copies ran while one was open for 13% of the time, Pallas kernels for 0%

commit v1 on v0

--- a/solution.py
+++ b/solution.py
@@ -56,12 +56,13 @@
         lower_ids,
         want_lower,
     )
-    up_sel = place_all(
-        empty_upper,
-        lax.all_gather(upper[None], ("row", "col"), axis=0, tiled=True),
-        upper_ids,
-        want_upper,
+    apply_the_entries = lambda x_in: jnp.concatenate(
+        lax.all_to_all(
+            jnp.stack([x_in for _ in range(lax.axis_size(("row", "col")))], 0), ("row", "col"), 0, 0
+        ),
+        0,
     )
+    up_sel = place_all(empty_upper, apply_the_entries(upper[None]), upper_ids, want_upper)
     schur = jnp.einsum("pkab,kqbc->pqac", low_sel, up_sel, preferred_element_type=jnp.float32)
     summed = lax.psum_scatter(
         schur.astype(jnp.bfloat16), "layer", scatter_dimension=2, tiled=True

time: 251 us -> 323 us (1.29)
  waiting for transfers between devices: 183 us -> 243 us
  starting transfers between devices: 0.12 us -> 12.4 us
  other arithmetic: 6.61 us -> 3.34 us
    all_to_all x0 -> x1, waiting for transfers between devices: none -> 200 us  [shards(): lax.all_to_all(jnp.stack([x_in for _ in range(lax.axis_size(('row', 'col'...]
    all_gather x1, waiting for transfers between devices: 75.3 us -> 0.01 us  [shards(): lax.all_gather(lower[None], ('row', 'col'), axis=0, tiled=True)]
    all_gather x1 -> x0, waiting for transfers between devices: 67.2 us -> none  [shards(): lax.all_gather(upper[None], ('row', 'col'), axis=0, tiled=True)]
    all_to_all x0 -> x1, starting transfers between devices: none -> 12.4 us  [shards(): lax.all_to_all(jnp.stack([x_in for _ in range(lax.axis_size(('row', 'col'...]
    another operation x0 -> x1, local copies, waits for them, and re-layouts: none -> 4.23 us  [shards(): jnp.stack([x_in for _ in range(lax.axis_size(('row', 'col')))], 0)]
    unnamed x4 -> x3, waiting for transfers between devices: 40.6 us -> 42.8 us
  transfers between devices with their start and end apart: 3 -> 3, of which waited for: 3 -> 2; matrix products, arithmetic and copies ran while one was open for 13% -> 5% of each run, Pallas kernels for 0% -> 0%
where the time goes in v1:
time: 323 us; the launch traced here: 322 us
  waiting for transfers between devices  243 us (75%)
  local copies, waits for them, and re-layouts  31.3 us (10%)
  between operations  19.4 us (6%)
  matrix products  12.6 us (4%)
  starting transfers between devices  12.4 us (4%)
  other arithmetic  3.34 us (1%)
    all_to_all x1, waiting for transfers between devices, shards(): lax.all_to_all(jnp.stack([x_in for _ in range(lax.axis_size(('row', 'col'...  200 us
    unnamed x3, waiting for transfers between devices  42.8 us
    all_to_all x1, starting transfers between devices, shards(): lax.all_to_all(jnp.stack([x_in for _ in range(lax.axis_size(('row', 'col'...  12.4 us
    all_gather x1, local copies, waits for them, and re-layouts, shards(): lax.all_gather(lower[None], ('row', 'col'), axis=0, tiled=True)  11.9 us
    gather x2, local copies, waits for them, and re-layouts, place_all(): picked = blocks[position]  10.8 us
  transfers between devices with their start and end apart: 3, of which 2 were waited for; matrix products, arithmetic and copies ran while one was open for 5% of the time, Pallas kernels for 0%

profile of v1, /device:TPU:2, one launch (start us, length us, event | category | flops | bytes accessed | tf_op | source)
XLA Modules:
  0.0 322.2 jit_solution(2612672614726233450)
XLA Ops:
  7.2 0.0 copy-start
  7.2 1.4 constant_dynamic-slice_fusion
  11.2 1.2 convolution_convert_fusion.1
  12.4 4.2 %stack.3 = bf16[64,1,256,256]{3,2,1,0:T(8,128)(2,1)} broadcast(bf16[256,256]{1,0:T(8,128)(2,1)S(1)} %convolution_convert_fusion.1), dimensions={2,3} | broadcast | bytes 8519680 | tf_op jit(solution)/shard_map/stack | solution.py:61
  16.6 0.0 copy-start.2
  16.6 0.0 copy-start.5
  16.6 0.0 copy-start.3
  16.6 0.0 copy-start.6
  16.6 0.0 copy-start.4
  16.6 0.0 copy-start.7
  16.6 12.4 %all-to-all-start = ((bf16[64,1,256,256]{3,2,1,0:T(8,128)(2,1)}), bf16[64,1,256,256]{3,2,1,0:T(8,128)(2,1)}, u32[]{:S(2)}, u32[]{:S(2)}) async-start(bf16[64,1,256,256]{3,2,1,0:T(8,128)(2,1)} %stack.3), calls=%async_computation | async-start | bytes 16777216 | tf_op jit(solution)/shard_map/all_to_all | solution.py:60
  29.0 0.0 all-gather.3.cloned.1.call-start
  31.0 0.0 copy-done.2
  31.0 1.8 fusion.29
  32.8 0.0 all-gather.3.cloned.1.call-update
  32.8 0.0 all-reduce.3.cloned.1.call-start
  32.9 0.0 copy-done.5
  32.9 0.1 dynamic_slice.19
  33.0 0.1 broadcast_add_fusion
  33.1 0.0 copy-done.3
  33.1 0.7 fusion.37
  33.8 0.1 copy.27
  33.9 0.1 reshape.76
  34.0 0.0 copy-done.6
  34.0 0.1 dynamic-slice_multiply_fusion
  34.1 0.1 iota_add_fusion
  34.1 0.0 copy-done.4
  34.1 0.8 fusion.38
  34.9 0.1 reshape.84
  35.0 0.2 compare_reduce_fusion.1
  35.2 0.1 copy.26
  35.3 0.0 copy-done.7
  35.3 0.6 dynamic-slice.2
  36.6 0.2 compare_reduce_fusion
  36.8 200.3 %all-to-all-done = bf16[64,1,256,256]{3,2,1,0:T(8,128)(2,1)} async-done(((bf16[64,1,256,256]{3,2,1,0:T(8,128)(2,1)}), bf16[64,1,256,256]{3,2,1,0:T(8,128)(2,1)}, u32[]{:S(2)}, u32[]{:S(2)}) %all-to-all-start) | async-done | bytes 8388640 | tf_op jit(solution)/shard_map/all_to_all | solution.py:60
  237.1 5.4 %gather_fusion = bf16[16,256,256]{2,1,0:T(8,128)(2,1)} fusion(bf16[64,256,256]{2,1,0:T(8,128)(2,1)} %bitcast.4, s32[1024]{0:T(1024)S(1)} %pad_clamp_fusion.1), kind=kCustom, calls=%fused_computation | custom fusion | bytes 4194368 | tf_op jit(solution)/shard_map/gather | solution.py:11
  242.5 11.9 %copy.37 = bf16[16384,256]{1,0:T(8,128)(2,1)} copy(bf16[16384,256]{0,1:T(8,128)(2,1)} %all-gather.3.cloned.1.call-done) | data formatting | bytes 16777216 | tf_op jit(solution)/shard_map/all_gather | solution.py:55
  254.3 5.4 %gather_fusion.1 = bf16[16,256,256]{2,1,0:T(8,128)(2,1)} fusion(bf16[64,256,256]{2,1,0:T(8,128)(2,1)} %bitcast.60, s32[1024]{0:T(1024)S(1)} %pad_clamp_fusion), kind=kCustom, calls=%fused_computation.1 | custom fusion | bytes 4194368 | tf_op jit(solution)/shard_map/gather | solution.py:11
  259.7 3.7 %fusion.24 = bf16[2,2,256,256]{2,3,0,1:T(8,128)(2,1)S(1)} fusion(bf16[2,8,256,256]{3,2,1,0:T(8,128)(2,1)} %bitcast.62, pred[2,8]{1,0:T(4,128)(4,1)S(1)} %compare_reduce_fusion, bf16[8,2,256,256]{3,2,1,0:T(8,128)(2,1)} %bitcast.61, pred[8,2]{1,0:T(8,128)(4,1)S(1)} %copy.26), kind=kOutput, calls=%fused_computation.16 | convolution fusion | flops 1076101120 | bytes 4718624 | tf_op jit(solution)/shard_map/pkab,kqbc->pqac/dot_general | solution.py:66
  263.4 1.2 copy.30
  264.6 0.0 all-reduce.3.cloned.1.call-update
  264.6 0.0 copy-done
  264.6 0.0 copy-start.1
  264.7 5.9 %fusion.1 = bf16[1,1024,1024]{2,1,0:T(8,128)(2,1)} fusion(bf16[1,1024,1024]{2,1,0:T(8,128)(2,1)} %param.23, bf16[1,1024,1024]{2,1,0:T(8,128)(2,1)S(1)} %copy-done, bf16[1,1024,1024]{2,1,0:T(8,128)(2,1)} %param.21), kind=kOutput, calls=%fused_computation.4 | convolution fusion | flops 2150629376 | bytes 8388608 | tf_op jit(solution)/shard_map/dot_general | solution.py:71
  270.6 42.8 %all-reduce.3.cloned.1.call-done = bf16[2,2,256,256]{3,1,0,2:T(2,128)(2,1)} async-done(((bf16[2,2,256,256]{3,1,0,2:T(2,128)(2,1)}), bf16[2,2,256,256]{3,1,0,2:T(2,128)(2,1)}) %all-reduce.3.cloned.1.call-update) | async-done | bytes 524304
  313.4 0.0 copy-done.1
  313.4 1.2 copy_subtract_fusion
  314.6 0.8 copy.32
  (6 shorter events, 0.0 us)
Async XLA Ops:
  7.2 257.5 %copy-start = (bf16[1,1024,1024]{2,1,0:T(8,128)(2,1)S(1)}, bf16[1,1024,1024]{2,1,0:T(8,128)(2,1)}, u32[]{:S(2)}) copy-start(bf16[1,1024,1024]{2,1,0:T(8,128)(2,1)} %param.22) | copy-start | bytes 6291460
  16.6 14.4 %copy-start.2 = (bf16[1,1,256,256]{3,2,1,0:T(8,128)(2,1)S(1)}, bf16[1,1,256,256]{3,2,1,0:T(8,128)(2,1)}, u32[]{:S(2)}) copy-start(bf16[1,1,256,256]{3,2,1,0:T(8,128)(2,1)} %param.12) | copy-start | bytes 393220
  16.6 16.3 %copy-start.5 = (s32[16]{0:T(128)S(1)}, s32[16]{0:T(128)}, u32[]{:S(2)}) copy-start(s32[16]{0:T(128)} %param.19) | copy-start | bytes 196
  16.6 16.5 %copy-start.3 = (s32[1,64]{1,0:T(1,128)S(1)}, s32[1,64]{1,0:T(1,128)}, u32[]{:S(2)}) copy-start(s32[1,64]{1,0:T(1,128)} %param.15) | copy-start | bytes 772
  16.6 17.4 %copy-start.6 = (s32[16]{0:T(128)S(1)}, s32[16]{0:T(128)}, u32[]{:S(2)}) copy-start(s32[16]{0:T(128)} %param.18) | copy-start | bytes 196
  16.6 17.5 %copy-start.4 = (s32[1,64]{1,0:T(1,128)S(1)}, s32[1,64]{1,0:T(1,128)}, u32[]{:S(2)}) copy-start(s32[1,64]{1,0:T(1,128)} %param.13) | copy-start | bytes 772
  16.6 18.7 %copy-start.7 = (u32[256]{0:T(256)S(1)}, u32[256]{0:T(256)}, u32[]{:S(2)}) copy-start(u32[256]{0:T(256)} %constant.79) | copy-start | bytes 3076
  16.6 220.4 %all-to-all-start = ((bf16[64,1,256,256]{3,2,1,0:T(8,128)(2,1)}), bf16[64,1,256,256]{3,2,1,0:T(8,128)(2,1)}, u32[]{:S(2)}, u32[]{:S(2)}) async-start(bf16[64,1,256,256]{3,2,1,0:T(8,128)(2,1)} %stack.3), calls=%async_computation | async-start | bytes 16777216 | tf_op jit(solution)/shard_map/all_to_all | solution.py:60
  29.0 213.5 %all-gather.3.cloned.1.call-start = ((), (), s32[]{:S(2)}) async-start(), calls=%async_computation.1 | async-start | bytes 8519680 | tf_op jit(solution)/shard_map/all_gather | solution.py:55
  32.8 280.6 %all-reduce.3.cloned.1.call-start = ((), (), s32[]{:S(2)}) async-start(), calls=%async_computation.2 | async-start | bytes 1048576
  264.6 48.7 %copy-start.1 = (f32[2,2,64,256]{3,2,1,0:T(8,128)S(1)}, f32[2,2,64,256]{3,2,1,0:T(8,128)}, u32[]{:S(2)}) copy-start(f32[2,2,64,256]{3,2,1,0:T(8,128)} %param.20) | copy-start | bytes 786436
Sparse Core Ops, SparseCore 0:
  33.0 181.0 all-gather.2
  264.8 48.5 all-reduce.2
